TPU v7x, 256 devices: a whole 4x4x8 slice. The times are simulated.
256 devices in a mesh: child: 2 (over y_hi), row: 32 (over z, y_lo, core), col: 4 (over x).
Axes of the slice: x: 4, y: 4 (y_hi: 2, y_lo: 2; y = y_hi * 2 + y_lo), z: 8, core: 2. Of those that a mesh axis runs over, the one named last changes fastest.
Arguments:
- front: bfloat16 [131072, 2048], P(('row', 'child'), 'col'), as said below
- left_factors: bfloat16 [2, 4, 64, 131072], P('child', 'col', None, 'row'), may hold values from -2.5 to 2.5
- right_factors: bfloat16 [2, 256, 64, 2048], P('child', 'row', None, 'col'), may hold values from -2.5 to 2.5
Outputs:
- panel_t: bfloat16 [2048, 131072], P('col', ('row', 'child'))
Inputs may be any that keep to these rules, and one draw needn't show every extreme that they name: The first 2048 rows of front make the symmetric part of the assembled diagonal block positive definite: its diagonal entries exceed the spectral norm of the rest of that part several times.
All inputs are finite; a program needn't handle non-finite values.
Results may differ from a plain program's by a relative error of at most 0.012.
Values may be sent and summed in bfloat16 or wider, within the bound.
No kernel may reach another device: no remote copies, remote signals or barrier semaphores. Data moves between devices by JAX's collectives and lax.ppermute only.
A program may use at most 128 MiB of HBM per device.

v0:
```python
import jax
import jax.numpy as jnp
from jax import lax
from jax.sharding import PartitionSpec as P

TILE = 512
RANK = 64
PW = 2048


def shortened(array):

    def short(part):
        return part.astype(jnp.bfloat16) if part.dtype == jnp.float32 else part

    return jax.tree.map(short, array)


def spread(value, axis, source):
    kept = jnp.where(lax.axis_index(axis) == source, value, 0).astype(value.dtype)
    return lax.psum(kept, axis)


def product_high(left, right):
    return jnp.dot(left, right, precision=lax.Precision.HIGHEST)


def inverse_transpose(top):
    blocks = PW // TILE
    identity = jnp.eye(TILE, dtype=jnp.float32)

    def tile_of(i, j):
        return top[i * TILE : (i + 1) * TILE, j * TILE : (j + 1) * TILE].astype(jnp.float32)

    def sym_tile(i, j):
        return 0.5 * (tile_of(i, j) + tile_of(j, i).T)

    lower = {}
    diag_inv = {}
    for j in range(blocks):
        accum = sym_tile(j, j)
        for k in range(j):
            accum = accum - product_high(lower[j, k], lower[j, k].T)
        lower[j, j] = jnp.linalg.cholesky(accum)
        diag_inv[j] = lax.linalg.triangular_solve(lower[j, j], identity, left_side=True, lower=True)
        for i in range(j + 1, blocks):
            accum = sym_tile(i, j)
            for k in range(j):
                accum = accum - product_high(lower[i, k], lower[j, k].T)
            lower[i, j] = product_high(accum, diag_inv[j].T)
    pieces = {}
    for i in range(blocks):
        pieces[i, i] = diag_inv[i]
    for i in range(blocks):
        for j in range(i):
            acc = jnp.zeros((TILE, TILE), jnp.float32)
            for k in range(j, i):
                acc = acc + product_high(lower[i, k], pieces[k, j])
            pieces[i, j] = -product_high(pieces[i, i], acc)
    zero_tile = jnp.zeros((TILE, TILE), jnp.bfloat16)
    row_list = [
        jnp.concatenate(
            [pieces[b, a].T.astype(jnp.bfloat16) if a <= b else zero_tile for b in range(blocks)],
            axis=1,
        )
        for a in range(blocks)
    ]
    return jnp.concatenate(row_list, axis=0)


def child_term(left_part, right_part):
    left_tiles = left_part.reshape(RANK, right_part.shape[0], TILE)
    result = jnp.einsum("rtk,trn->tkn", left_tiles, right_part, preferred_element_type=jnp.float32)
    return result.reshape(-1, TILE)


def shards(front, left_factors, right_factors):
    side = lax.axis_index("child")
    left_all = left_factors[0, 0]
    right_all = right_factors[0]
    update = lax.psum_scatter(
        child_term(left_all, right_all).astype(jnp.bfloat16),
        "child",
        scatter_dimension=0,
        tiled=True,
    ).astype(jnp.float32)
    panel_rows = (front.astype(jnp.float32) - update).astype(jnp.bfloat16)
    column = lax.axis_index("col")
    is_root = jnp.logical_and(side == 0, lax.axis_index("row") == 0)
    top = lax.all_gather(panel_rows[:PW], "col", axis=1, tiled=True)

    def select_block(matrix):
        return lax.dynamic_slice_in_dim(matrix, column * TILE, TILE, 0)

    empty_shape = (TILE, PW)
    local_block = lax.cond(
        is_root,
        lambda t: select_block(inverse_transpose(t)),
        lambda t: jnp.zeros(empty_shape, jnp.bfloat16),
        top,
    )
    inverse_block = jax.tree.map(
        lambda part, own: part.astype(own.dtype),
        jax.tree.map(lambda part: spread(part, ("child", "row"), 0), shortened(local_block)),
        local_block,
    )
    part = lax.slice_in_dim(inverse_block, 0, lax.axis_size("col") * TILE, axis=1)
    panel_t = lax.psum_scatter(
        lax.dot_general(
            part, panel_rows, (((0,), (1,)), ((), ())), preferred_element_type=jnp.float32
        ),
        "col",
        scatter_dimension=0,
        tiled=True,
    )
    return panel_t.astype(jnp.bfloat16)


def solution(mesh):
    in_specs = (
        P(("row", "child"), "col"),
        P("child", "col", None, "row"),
        P("child", "row", None, "col"),
    )
    out_specs = P("col", ("row", "child"))
    return jax.shard_map(shards, mesh=mesh, in_specs=in_specs, out_specs=out_specs, check_vma=False)
```

profile of v0, /device:TPU:1, one launch (start us, length us, event | category | flops | bytes accessed | tf_op | source)
XLA Modules:
  0.0 1288.6 jit_solution(6734739488787908376)
XLA Ops:
  6.5 0.0 copy-start
  6.5 0.0 reduce-scatter.3.cloned.1.call-start
  6.5 1.3 copy.31
  7.8 0.0 copy-done
  7.8 0.0 copy-start.46
  7.8 3.2 convolution_convert_fusion
  11.1 0.0 reduce-scatter.3.cloned.1.call-update
  11.1 0.0 all-gather.2.cloned.1.call-start
  11.1 64.8 %reduce-scatter.3.cloned.1.call-done = bf16[2048,512]{1,0:T(8,128)(2,1)} async-done(((bf16[4096,512]{1,0:T(8,128)(2,1)}), bf16[2048,512]{1,0:T(8,128)(2,1)}) %reduce-scatter.3.cloned.1.call-update) | async-done | bytes 2097168 | tf_op jit(solution)/shard_map/reduce_scatter | solution.py:81
  76.0 0.0 copy-done.46
  76.0 3.5 subtract_convert_fusion
  79.5 0.0 all-gather.2.cloned.1.call-update
  79.5 0.0 all-reduce.4.cloned.1.call-start
  79.5 85.1 %all-gather.2.cloned.1.call-done = bf16[2048,2048]{1,0:T(8,128)(2,1)} async-done(((bf16[2048,512]{1,0:T(8,128)(2,1)}), bf16[2048,2048]{1,0:T(8,128)(2,1)}) %all-gather.2.cloned.1.call-update) | async-done | bytes 8388624 | tf_op jit(solution)/shard_map/all_gather | solution.py:90
  164.7 1.5 conditional.1
  164.7 1.5 broadcast.134
  166.2 0.0 copy-start.35
  166.2 1.5 broadcast_select_fusion
  167.7 0.0 all-reduce.4.cloned.1.call-update
  167.7 0.0 reduce-scatter.5.cloned.1.call-start
  167.8 949.7 %all-reduce.4.cloned.1.call-done = bf16[512,2048]{0,1:T(8,128)(2,1)} async-done(((bf16[512,2048]{0,1:T(8,128)(2,1)}), bf16[512,2048]{0,1:T(8,128)(2,1)}) %all-reduce.4.cloned.1.call-update) | async-done | bytes 2097168 | tf_op jit(solution)/shard_map/psum | solution.py:21
  1117.5 0.0 copy-done.35
  1117.5 9.7 fusion.185
  1127.2 0.0 reduce-scatter.5.cloned.1.call-update
  1127.2 0.0 copy-start.1
  1127.2 151.0 %reduce-scatter.5.cloned.1.call-done = f32[512,2048]{1,0:T(8,128)} async-done(((f32[2048,2048]{1,0:T(8,128)}), f32[512,2048]{1,0:T(8,128)}) %reduce-scatter.5.cloned.1.call-update) | async-done | bytes 4194320 | tf_op jit(solution)/shard_map/reduce_scatter | solution.py:108
  1278.2 3.8 convert_element_type.129
  1282.1 0.0 copy-done.1
Async XLA Ops:
  6.5 1.3 copy-start
  6.5 69.4 %reduce-scatter.3.cloned.1.call-start = ((), (), s32[]{:S(2)}) async-start(), calls=%async_computation.2 | async-start | bytes 6291456 | tf_op jit(solution)/shard_map/reduce_scatter | solution.py:81
  7.8 68.1 %copy-start.46 = (bf16[2048,512]{1,0:T(8,128)(2,1)S(1)}, bf16[2048,512]{1,0:T(8,128)(2,1)}, u32[]{:S(2)}) copy-start(bf16[2048,512]{1,0:T(8,128)(2,1)} %param.8) | copy-start | bytes 6291460
  11.1 153.6 %all-gather.2.cloned.1.call-start = ((), (), s32[]{:S(2)}) async-start(), calls=%async_computation.3 | async-start | bytes 10485760 | tf_op jit(solution)/shard_map/all_gather | solution.py:90
  79.5 1038.0 %all-reduce.4.cloned.1.call-start = ((), (), s32[]{:S(2)}) async-start(), calls=%async_computation.4 | async-start | bytes 4194304 | tf_op jit(solution)/shard_map/psum | solution.py:21
  166.2 951.3 %copy-start.35 = (bf16[2048,512]{1,0:T(8,128)(2,1)S(1)}, bf16[2048,512]{1,0:T(8,128)(2,1)}, u32[]{:S(2)}) copy-start(bf16[2048,512]{1,0:T(8,128)(2,1)} %subtract_convert_fusion) | copy-start | bytes 6291460
  167.7 1110.5 %reduce-scatter.5.cloned.1.call-start = ((), (), s32[]{:S(2)}) async-start(), calls=%async_computation.5 | async-start | bytes 20971520 | tf_op jit(solution)/shard_map/reduce_scatter | solution.py:108
  1127.2 154.8 %copy-start.1 = (bf16[1,8,64,512]{3,2,1,0:T(8,128)(2,1)S(1)}, bf16[1,8,64,512]{3,2,1,0:T(8,128)(2,1)}, u32[]{:S(2)}) copy-start(bf16[1,8,64,512]{3,2,1,0:T(8,128)(2,1)} %param.10) | copy-start | bytes 1572868
Sparse Core Ops, SparseCore 0:
  11.2 64.6 reduce-scatter.2
  79.6 85.0 all-gather.1
  168.5 948.9 all-reduce.3
  1127.3 150.8 reduce-scatter.4
where the time goes:
time: 1290 us
  waiting for transfers between devices  1250 us (97%)
  between operations  13.2 us (1%)
  matrix products  12.9 us (1%)
    psum x1, waiting for transfers between devices, spread(): return lax.psum(kept, axis)  950 us
    reduce_scatter x1, waiting for transfers between devices, shards(): lax.psum_scatter(lax.dot_general(part, panel_rows, (((0,), (1,)), ((), ()...  151 us
    all_gather x1, waiting for transfers between devices, shards(): top = lax.all_gather(panel_rows[:PW], 'col', axis=1, tiled=True)  85.1 us
    reduce_scatter x1, waiting for transfers between devices, shards(): lax.psum_scatter(child_term(left_all, right_all).astype(jnp.bfloat16), 'c...  64.8 us
  transfers between devices with their start and end apart: 4, of which 4 were waited for; matrix products, arithmetic and copies ran while one was open for 0% of the time, Pallas kernels for 0%

commit v1 on v0

--- a/solution.py
+++ b/solution.py
@@ -87,7 +87,11 @@
     panel_rows = (front.astype(jnp.float32) - update).astype(jnp.bfloat16)
     column = lax.axis_index("col")
     is_root = jnp.logical_and(side == 0, lax.axis_index("row") == 0)
-    top = lax.all_gather(panel_rows[:PW], "col", axis=1, tiled=True)
+    t0 = panel_rows[:PW]
+    t1 = lax.axis_size("col")
+    arr_out = jnp.stack([t0] * t1)
+    heard = lax.all_to_all(arr_out, "col", 0, 0)
+    top = jnp.concatenate(heard, 1)
 
     def select_block(matrix):
         return lax.dynamic_slice_in_dim(matrix, column * TILE, TILE, 0)

time: 1290 us -> 1330 us (1.031)
  waiting for transfers between devices: 1250 us -> 1280 us
    all_to_all x0 -> x1, waiting for transfers between devices: none -> 93.1 us  [shards(): heard = lax.all_to_all(arr_out, 'col', 0, 0)]
    all_gather x1 -> x0, waiting for transfers between devices: 85.1 us -> none  [shards(): top = lax.all_gather(panel_rows[:PW], 'col', axis=1, tiled=True)]
    psum x1, waiting for transfers between devices: 950 us -> 974 us  [spread(): return lax.psum(kept, axis)]
where the time goes in v1:
time: 1330 us
  waiting for transfers between devices  1280 us (96%)
    psum x1, waiting for transfers between devices, spread(): return lax.psum(kept, axis)  974 us
    reduce_scatter x1, waiting for transfers between devices, shards(): lax.psum_scatter(lax.dot_general(part, panel_rows, (((0,), (1,)), ((), ()...  151 us
    all_to_all x1, waiting for transfers between devices, shards(): heard = lax.all_to_all(arr_out, 'col', 0, 0)  93.1 us
    reduce_scatter x1, waiting for transfers between devices, shards(): lax.psum_scatter(child_term(left_all, right_all).astype(jnp.bfloat16), 'c...  64.9 us
  transfers between devices with their start and end apart: 4, of which 4 were waited for; matrix products, arithmetic and copies ran while one was open for 0% of the time, Pallas kernels for 0%

profile of v1, /device:TPU:1, one launch (start us, length us, event | category | flops | bytes accessed | tf_op | source)
XLA Modules:
  0.0 1330.5 jit_solution(16687574312937381295)
XLA Ops:
  6.5 0.0 copy-start
  6.5 0.0 reduce-scatter.3.cloned.1.call-start
  6.5 1.3 copy.109
  7.8 0.0 copy-done
  7.8 0.0 copy-start.43
  7.8 3.2 convolution_convert_fusion
  11.1 0.0 reduce-scatter.3.cloned.1.call-update
  11.1 64.9 %reduce-scatter.3.cloned.1.call-done = bf16[2048,512]{1,0:T(8,128)(2,1)} async-done(((bf16[4096,512]{1,0:T(8,128)(2,1)}), bf16[2048,512]{1,0:T(8,128)(2,1)}) %reduce-scatter.3.cloned.1.call-update) | async-done | bytes 2097168 | tf_op jit(solution)/shard_map/reduce_scatter | solution.py:81
  76.0 0.0 copy-done.43
  76.0 2.2 subtract_convert_fusion
  78.1 0.0 copy-start.31
  78.1 1.3 copy-done.31
  79.5 4.0 stack.2
  83.5 5.6 all-to-all-start
  89.1 0.0 all-reduce.4.cloned.1.call-start
  89.2 93.1 %all-to-all-done = bf16[4,2048,512]{2,1,0:T(8,128)(2,1)} async-done(((bf16[4,2048,512]{2,1,0:T(8,128)(2,1)}), bf16[4,2048,512]{2,1,0:T(8,128)(2,1)}, u32[]{:S(2)}, u32[]{:S(2)}) %all-to-all-start) | async-done | bytes 8388640 | tf_op jit(solution)/shard_map/all_to_all | solution.py:93
  182.3 1.5 conditional.1
  182.3 1.5 broadcast.136
  183.7 0.0 copy-start.32
  183.7 1.5 broadcast_select_fusion
  185.2 0.0 all-reduce.4.cloned.1.call-update
  185.2 0.0 reduce-scatter.5.cloned.1.call-start
  185.3 974.1 %all-reduce.4.cloned.1.call-done = bf16[512,2048]{0,1:T(8,128)(2,1)} async-done(((bf16[512,2048]{0,1:T(8,128)(2,1)}), bf16[512,2048]{0,1:T(8,128)(2,1)}) %all-reduce.4.cloned.1.call-update) | async-done | bytes 2097168 | tf_op jit(solution)/shard_map/psum | solution.py:21
  1159.4 0.0 copy-done.32
  1159.4 9.7 fusion.181
  1169.1 0.0 reduce-scatter.5.cloned.1.call-update
  1169.1 0.0 copy-start.1
  1169.1 151.0 %reduce-scatter.5.cloned.1.call-done = f32[512,2048]{1,0:T(8,128)} async-done(((f32[2048,2048]{1,0:T(8,128)}), f32[512,2048]{1,0:T(8,128)}) %reduce-scatter.5.cloned.1.call-update) | async-done | bytes 4194320 | tf_op jit(solution)/shard_map/reduce_scatter | solution.py:112
  1320.1 3.8 convert_element_type.129
  1323.9 0.0 copy-done.1
Async XLA Ops:
  6.5 1.3 copy-start
  6.5 69.4 %reduce-scatter.3.cloned.1.call-start = ((), (), s32[]{:S(2)}) async-start(), calls=%async_computation.3 | async-start | bytes 6291456 | tf_op jit(solution)/shard_map/reduce_scatter | solution.py:81
  7.8 68.1 %copy-start.43 = (bf16[2048,512]{1,0:T(8,128)(2,1)S(1)}, bf16[2048,512]{1,0:T(8,128)(2,1)}, u32[]{:S(2)}) copy-start(bf16[2048,512]{1,0:T(8,128)(2,1)} %param.8) | copy-start | bytes 6291460
  78.1 1.4 copy-start.31
  83.5 98.8 %all-to-all-start = ((bf16[4,2048,512]{2,1,0:T(8,128)(2,1)}), bf16[4,2048,512]{2,1,0:T(8,128)(2,1)}, u32[]{:S(2)}, u32[]{:S(2)}) async-start(bf16[4,2048,512]{2,1,0:T(8,128)(2,1)} %stack.2), calls=%async_computation.1 | async-start | bytes 16777216 | tf_op jit(solution)/shard_map/all_to_all | solution.py:93
  89.1 1070.3 %all-reduce.4.cloned.1.call-start = ((), (), s32[]{:S(2)}) async-start(), calls=%async_computation.4 | async-start | bytes 4194304 | tf_op jit(solution)/shard_map/psum | solution.py:21
  183.7 975.7 %copy-start.32 = (bf16[2048,512]{1,0:T(8,128)(2,1)S(1)}, bf16[2048,512]{1,0:T(8,128)(2,1)}, u32[]{:S(2)}) copy-start(bf16[2048,512]{1,0:T(8,128)(2,1)} %copy-done.31) | copy-start | bytes 6291460
  185.2 1134.9 %reduce-scatter.5.cloned.1.call-start = ((), (), s32[]{:S(2)}) async-start(), calls=%async_computation.5 | async-start | bytes 20971520 | tf_op jit(solution)/shard_map/reduce_scatter | solution.py:112
  1169.1 154.8 %copy-start.1 = (bf16[1,8,64,512]{3,2,1,0:T(8,128)(2,1)S(1)}, bf16[1,8,64,512]{3,2,1,0:T(8,128)(2,1)}, u32[]{:S(2)}) copy-start(bf16[1,8,64,512]{3,2,1,0:T(8,128)(2,1)} %param.10) | copy-start | bytes 1572868
Sparse Core Ops, SparseCore 0:
  11.2 64.6 reduce-scatter.2
  185.3 974.0 all-reduce.3
  1169.2 150.8 reduce-scatter.4
